TPU v7x, 32 devices: a whole 2x2x4 slice. The times are simulated.
32 devices in a mesh: lat: 8 (over y, x, core), lon: 4 (over z).
Axes of the slice: x: 2, y: 2, z: 4, core: 2. Of those that a mesh axis runs over, the one named last changes fastest.
Arguments:
- tracer: float32 [16, 64, 2880], P(None, 'lat', 'lon'), may hold values from -6 to 6
- zonal_courant: float32 [16, 64, 2880], P(None, 'lat', 'lon'), may hold values from -0.35 to 0.35
- north_courant: float32 [16, 64, 2880], P(None, 'lat', 'lon'), may hold values from -0.35 to 0.35
- cutoff: int32 [16], replicated, may hold values from 1 to 128
Outputs:
- advanced: float32 [16, 64, 2880], P(None, 'lat', 'lon')
All inputs are finite; a program needn't handle non-finite values.
Results may differ from a plain program's by a relative error of at most 0.0001.
Values sent between devices are 32-bit elements; how exact they have to be, the bound alone decides.
A program may use at most 64 MiB of HBM per device.

v0:
```python
import math
import jax
import jax.numpy as jnp
from jax import lax
from jax.sharding import PartitionSpec as P

NLON = 2880
KMAX = 128
DIFFUSION = 0.2


def with_halo(block, sides, width, periodic):
    for axis, dim in sides:
        count = lax.axis_size(axis)
        forward = [(i, i + 1) for i in range(count - 1)]
        if periodic:
            forward.append((count - 1, 0))
        backward = [(target, source) for source, target in forward]
        low = lax.ppermute(
            lax.slice_in_dim(block, block.shape[dim] - width, None, axis=dim), axis, forward
        )
        high = lax.ppermute(lax.slice_in_dim(block, 0, width, axis=dim), axis, backward)
        block = jnp.concatenate([low, block, high], axis=dim)
    return block


def shifted(block, axis, distance):
    devices = range(lax.axis_size(axis))
    route = [((i - distance) % len(devices), i) for i in devices]
    return lax.ppermute(block, axis, route)


def fourier_tables(columns):
    modes = jnp.arange(KMAX, dtype=jnp.int32)
    product = columns[:, None] * modes[None, :] % NLON
    phase_angle = product.astype(jnp.float32) * (2.0 * math.pi / NLON)
    weights = jnp.where(modes == 0, 1.0 / NLON, 2.0 / NLON).astype(jnp.float32)
    cosine = jnp.cos(phase_angle)
    sine = jnp.sin(phase_angle)
    analysis = jnp.concatenate([cosine * weights[None, :], sine * weights[None, :]], axis=1)
    synthesis = jnp.concatenate([cosine, sine], axis=1).T
    return (analysis, synthesis)


def mode_mask(cut_values):
    modes = jnp.arange(KMAX, dtype=jnp.float32)
    doubled = jnp.concatenate([modes, modes])
    return (doubled[None, :] < cut_values[:, None]).astype(jnp.float32)


def shards(tracer, zonal_courant, north_courant, cutoff):
    level_count, row_count, col_count = tracer.shape
    lat_count = lax.axis_size("lat")
    lon_count = lax.axis_size("lon")
    lat_at = lax.axis_index("lat")
    lon_at = lax.axis_index("lon")
    cap_blocks = lat_count // 8
    polar = (lat_at < cap_blocks) | (lat_at >= lat_count - cap_blocks)
    offset = jnp.where(
        lat_at < cap_blocks,
        lat_at * row_count,
        jnp.where(polar, (lat_at - lat_count + 2 * cap_blocks) * row_count, 0),
    )
    row_cut = lax.dynamic_slice_in_dim(cutoff, offset, row_count).astype(jnp.float32)
    flat_count = level_count * row_count
    flat_cut = jnp.broadcast_to(row_cut[None, :], (level_count, row_count)).reshape(flat_count)
    local_columns = lon_at * col_count + jnp.arange(col_count, dtype=jnp.int32)
    analysis, synthesis = fourier_tables(local_columns)
    state = tracer
    for substep in range(2):
        padded = with_halo(state, (("lat", 1),), 1, False)
        edge_rows = jnp.concatenate([state[:, :1], state[:, -1:]], axis=1)
        opposite = shifted(edge_rows, "lon", lon_count // 2)
        south_rim = jnp.where(lat_at == 0, opposite[:, 0], padded[:, 0])
        north_rim = jnp.where(lat_at == lat_count - 1, opposite[:, 1], padded[:, -1])
        padded = jnp.concatenate([south_rim[:, None], padded[:, 1:-1], north_rim[:, None]], axis=1)
        padded = with_halo(padded, (("lon", 2),), 1, True)
        center = padded[:, 1:-1, 1:-1]
        east_cell = padded[:, 1:-1, 2:]
        west_cell = padded[:, 1:-1, :-2]
        north_cell = padded[:, 2:, 1:-1]
        south_cell = padded[:, :-2, 1:-1]
        tendency = (
            -0.5 * zonal_courant * (east_cell - west_cell)
            - 0.5 * north_courant * (north_cell - south_cell)
            + DIFFUSION * (east_cell + west_cell + north_cell + south_cell - 4.0 * center)
        )
        flat_rows = tendency.reshape(flat_count, col_count)
        partial_coeffs = jnp.dot(flat_rows, analysis, precision=lax.Precision.HIGHEST)
        coefficients = lax.psum(partial_coeffs, "lon")
        coefficients = coefficients * mode_mask(flat_cut)
        filtered = jnp.dot(coefficients, synthesis, precision=lax.Precision.HIGHEST)
        filtered = filtered.reshape(level_count, row_count, col_count)
        state = state + jnp.where(polar, filtered, tendency)
    return state


def solution(mesh):
    return jax.shard_map(
        shards,
        mesh=mesh,
        in_specs=(P(None, "lat", "lon"), P(None, "lat", "lon"), P(None, "lat", "lon"), P()),
        out_specs=P(None, "lat", "lon"),
        check_vma=False,
    )
```

profile of v0, /device:TPU:0, one launch (start us, length us, event | category | flops | bytes accessed | tf_op | source)
XLA Modules:
  0.0 136.2 jit_solution(5212779486867433260)
XLA Ops:
  6.5 1.2 fusion.28
  7.7 2.4 %collective-permute-start.1 = (f32[16,1,720]{2,1,0:T(1,128)S(1)}, f32[16,1,720]{2,1,0:T(1,128)S(1)}, u32[]{:S(2)}, u32[]{:S(2)}) collective-permute-start(f32[16,1,720]{2,1,0:T(1,128)S(1)} %get-tuple-element.11), channel_id=1, source_target_pairs={{0,4},{4,8},{8,12},{12,16},{16,20},{20,24},{24,28},{1,5},{5,9},{9,... | collective-permute-start | bytes 138248 | tf_op jit(solution)/shard_map/ppermute | solution.py:19
  10.1 1.3 collective-permute-start.2
  11.5 3.5 %collective-permute-start = (f32[16,2,720]{2,1,0:T(2,128)S(1)}, f32[16,2,720]{2,1,0:T(2,128)S(1)}, u32[]{:S(2)}, u32[]{:S(2)}) collective-permute-start(f32[16,2,720]{2,1,0:T(2,128)S(1)} %pad_maximum_fusion.28), channel_id=1, source_target_pairs={{2,0},{3,1},{0,2},{1,3},{6,4},{7,5},{4,6},{5,7},{10,8},{11,9},{8,1... | collective-permute-start | bytes 276488 | tf_op jit(solution)/shard_map/ppermute | solution.py:30
  15.0 1.6 %broadcast_multiply_fusion.1 = (f32[720,128]{1,0:T(8,128)S(1)}, f32[720,128]{1,0:T(8,128)S(1)}, f32[720,128]{1,0:T(8,128)S(1)}, f32[720,128]{1,0:T(8,128)S(1)}) fusion(f32[128]{0:T(128)S(1)} %compare_select_fusion.4, s32[720]{0:T(1024)S(1)} %iota_add_fusion), kind=kLoop, calls=%fused_computation.40 | loop fusion | flops 1013760 | bytes 1477952 | tf_op jit(solution)/shard_map/mul | solution.py:40
  16.7 0.9 collective-permute-done
  17.6 0.1 broadcast_select_fusion.3
  17.8 0.1 pad_maximum_fusion.25
  17.9 3.8 %collective-permute-start.4 = (f32[16,10,1]{2,1,0:T(8,128)S(1)}, f32[16,10,1]{2,1,0:T(8,128)S(1)}, u32[]{:S(2)}, u32[]{:S(2)}) collective-permute-start(f32[16,10,1]{2,1,0:T(8,128)S(1)} %get-tuple-element.7), channel_id=1, source_target_pairs={{0,1},{1,2},{2,3},{3,0},{4,5},{5,6},{6,7},{7,4},{8,9},{9,10},{10,1... | collective-permute-start | bytes 1928 | tf_op jit(solution)/shard_map/ppermute | solution.py:19
  21.7 2.9 %collective-permute-start.3 = (f32[16,10,1]{2,1,0:T(8,128)S(1)}, f32[16,10,1]{2,1,0:T(8,128)}, u32[]{:S(2)}, u32[]{:S(2)}) collective-permute-start(f32[16,10,1]{2,1,0:T(8,128)S(1)} %get-tuple-element.8), channel_id=1, source_target_pairs={{1,0},{2,1},{3,2},{0,3},{5,4},{6,5},{7,6},{4,7},{9,8},{10,9},{11,1... | collective-permute-start | bytes 1928 | tf_op jit(solution)/shard_map/ppermute | solution.py:22
  24.6 4.3 %collective-permute-done.4 = f32[16,10,1]{2,1,0:T(8,128)S(1)} collective-permute-done((f32[16,10,1]{2,1,0:T(8,128)S(1)}, f32[16,10,1]{2,1,0:T(8,128)S(1)}, u32[]{:S(2)}, u32[]{:S(2)}) %collective-permute-start.4) | collective-permute-done | bytes 672 | tf_op jit(solution)/shard_map/ppermute | solution.py:19
  28.9 0.7 copy-done.3
  29.6 0.7 collective-permute-done.3
  30.3 1.6 %multiply_add_fusion.1 = f32[16,8,720]{2,1,0:T(8,128)S(1)} fusion(f32[16,8,720]{2,1,0:T(8,128)S(1)} %copy-done, f32[16,1,720]{2,1,0:T(1,128)S(1)} %get-tuple-element.16, f32[16,1,720]{2,1,0:T(1,128)S(1)} %get-tuple-element.15, f32[16,10,1]{2,1,0:T(8,128)} %collective-permute-done.3, f32[16,10,1]{2,1,0:T(8,128)} %copy-done.3, f32[16,8,720]{2,1,0:T(8,128)S(1)} %copy-done.1, ...), kind=kLoop, calls=%fused_computation.30 | loop fusion | flops 2027520 | bytes 1568000 | tf_op jit(solution)/shard_map/add | solution.py:84
  31.8 1.2 fusion.5
  33.1 0.6 copy-done.4
  33.9 35.7 %all-reduce.3.cloned.1.call-done = f32[128,256]{1,0:T(8,128)} async-done(((f32[128,256]{1,0:T(8,128)}), f32[128,256]{1,0:T(8,128)}) %all-reduce.3.cloned.1.call-update) | async-done | bytes 131088 | tf_op jit(solution)/shard_map/psum | solution.py:90
  69.5 1.7 %fusion.1 = f32[16,8,720]{2,1,0:T(8,128)S(1)} fusion(f32[16,8,720]{2,1,0:T(8,128)S(1)} %copy-done, f32[16,8,720]{2,1,0:T(8,128)S(1)} %multiply_add_fusion.1, f32[720,128]{1,0:T(8,128)S(1)} %get-tuple-element.19, f32[720,128]{1,0:T(8,128)S(1)} %get-tuple-element.20, pred[]{:T(512)S(6)} %or.3, f32[128,256]{1,0:T(8,128)} %all-reduce.3.cloned.1.call-done, ...), kind=kOutput, calls=%fused_computation.3 | convolution fusion | flops 283549696 | bytes 1975809 | tf_op jit(solution)/shard_map/dot_general | solution.py:92
  71.4 2.1 %collective-permute-start.5 = (f32[16,2,720]{2,1,0:T(2,128)S(1)}, f32[16,2,720]{2,1,0:T(2,128)S(1)}, u32[]{:S(2)}, u32[]{:S(2)}) collective-permute-start(f32[16,2,720]{2,1,0:T(2,128)S(1)} %pad_maximum_fusion.29), channel_id=1, source_target_pairs={{2,0},{3,1},{0,2},{1,3},{6,4},{7,5},{4,6},{5,7},{10,8},{11,9},{8,1... | collective-permute-start | bytes 276488 | tf_op jit(solution)/shard_map/ppermute | solution.py:30
  73.6 1.3 collective-permute-start.6
  74.9 1.3 collective-permute-start.7
  76.2 3.5 %collective-permute-done.7 = f32[16,1,720]{2,1,0:T(1,128)S(1)} collective-permute-done((f32[16,1,720]{2,1,0:T(1,128)S(1)}, f32[16,1,720]{2,1,0:T(1,128)S(1)}, u32[]{:S(2)}, u32[]{:S(2)}) %collective-permute-start.7) | collective-permute-done | bytes 46112 | tf_op jit(solution)/shard_map/ppermute | solution.py:22
  79.7 0.1 broadcast_select_fusion.2
  79.8 0.1 pad_maximum_fusion.22
  80.0 0.6 collective-permute-start.9
  80.6 3.3 %collective-permute-start.8 = (f32[16,10,1]{2,1,0:T(8,128)S(1)}, f32[16,10,1]{2,1,0:T(8,128)S(1)}, u32[]{:S(2)}, u32[]{:S(2)}) collective-permute-start(f32[16,10,1]{2,1,0:T(8,128)S(1)} %get-tuple-element.6), channel_id=1, source_target_pairs={{1,0},{2,1},{3,2},{0,3},{5,4},{6,5},{7,6},{4,7},{9,8},{10,9},{11,1... | collective-permute-start | bytes 1928 | tf_op jit(solution)/shard_map/ppermute | solution.py:22
  83.9 3.0 %collective-permute-done.9 = f32[16,10,1]{2,1,0:T(8,128)S(1)} collective-permute-done((f32[16,10,1]{2,1,0:T(8,128)S(1)}, f32[16,10,1]{2,1,0:T(8,128)S(1)}, u32[]{:S(2)}, u32[]{:S(2)}) %collective-permute-start.9) | collective-permute-done | bytes 672 | tf_op jit(solution)/shard_map/ppermute | solution.py:19
  86.9 0.1 collective-permute-done.8
  87.0 0.6 multiply_add_fusion
  87.7 1.2 fusion.4
  88.9 38.0 %all-reduce.5.cloned.1.call-done = f32[128,256]{1,0:T(8,128)} async-done(((f32[128,256]{1,0:T(8,128)}), f32[128,256]{1,0:T(8,128)}) %all-reduce.5.cloned.1.call-update) | async-done | bytes 131088 | tf_op jit(solution)/shard_map/psum | solution.py:90
  126.9 2.5 %fusion.3 = f32[16,8,720]{2,1,0:T(8,128)} fusion(f32[16,8,720]{2,1,0:T(8,128)S(1)} %fusion.1, f32[16,8,720]{2,1,0:T(8,128)S(1)} %multiply_add_fusion, f32[720,128]{1,0:T(8,128)S(1)} %get-tuple-element.19, f32[720,128]{1,0:T(8,128)S(1)} %get-tuple-element.20, pred[]{:T(512)S(6)} %or.3, f32[128,256]{1,0:T(8,128)} %all-reduce.5.cloned.1.call-done, ...), kind=kOutput, calls=%fused_computation.5 | convolution fusion | flops 283549696 | bytes 1975809 | tf_op jit(solution)/shard_map/dot_general | solution.py:92
  (26 shorter events, 0.5 us)
Async XLA Ops:
  6.5 63.0 %all-reduce.3.cloned.1.call-start = ((), (), s32[]{:S(2)}) async-start(), calls=%async_computation | async-start | bytes 262144 | tf_op jit(solution)/shard_map/psum | solution.py:90
  7.7 8.9 %collective-permute-start.1 = (f32[16,1,720]{2,1,0:T(1,128)S(1)}, f32[16,1,720]{2,1,0:T(1,128)S(1)}, u32[]{:S(2)}, u32[]{:S(2)}) collective-permute-start(f32[16,1,720]{2,1,0:T(1,128)S(1)} %get-tuple-element.11), channel_id=1, source_target_pairs={{0,4},{4,8},{8,12},{12,16},{16,20},{20,24},{24,28},{1,5},{5,9},{9,... | collective-permute-start | bytes 138248 | tf_op jit(solution)/shard_map/ppermute | solution.py:19
  10.1 6.5 %collective-permute-start.2 = (f32[16,1,720]{2,1,0:T(1,128)S(1)}, f32[16,1,720]{2,1,0:T(1,128)S(1)}, u32[]{:S(2)}, u32[]{:S(2)}) collective-permute-start(f32[16,1,720]{2,1,0:T(1,128)S(1)} %get-tuple-element.12), channel_id=1, source_target_pairs={{4,0},{8,4},{12,8},{16,12},{20,16},{24,20},{28,24},{5,1},{9,5},{13... | collective-permute-start | bytes 138248 | tf_op jit(solution)/shard_map/ppermute | solution.py:22
  11.5 6.1 %collective-permute-start = (f32[16,2,720]{2,1,0:T(2,128)S(1)}, f32[16,2,720]{2,1,0:T(2,128)S(1)}, u32[]{:S(2)}, u32[]{:S(2)}) collective-permute-start(f32[16,2,720]{2,1,0:T(2,128)S(1)} %pad_maximum_fusion.28), channel_id=1, source_target_pairs={{2,0},{3,1},{0,2},{1,3},{6,4},{7,5},{4,6},{5,7},{10,8},{11,9},{8,1... | collective-permute-start | bytes 276488 | tf_op jit(solution)/shard_map/ppermute | solution.py:30
  15.0 2.7 %copy-start = (f32[16,8,720]{2,1,0:T(8,128)S(1)}, f32[16,8,720]{2,1,0:T(8,128)}, u32[]{:S(2)}) copy-start(f32[16,8,720]{2,1,0:T(8,128)} %param.4) | copy-start | bytes 1105924
  17.6 12.7 %copy-start.2 = (f32[16,8,720]{2,1,0:T(8,128)S(1)}, f32[16,8,720]{2,1,0:T(8,128)}, u32[]{:S(2)}) copy-start(f32[16,8,720]{2,1,0:T(8,128)} %param.5) | copy-start | bytes 1105924
  17.7 12.5 %copy-start.1 = (f32[16,8,720]{2,1,0:T(8,128)S(1)}, f32[16,8,720]{2,1,0:T(8,128)}, u32[]{:S(2)}) copy-start(f32[16,8,720]{2,1,0:T(8,128)} %param.6) | copy-start | bytes 1105924
  17.9 11.0 %collective-permute-start.4 = (f32[16,10,1]{2,1,0:T(8,128)S(1)}, f32[16,10,1]{2,1,0:T(8,128)S(1)}, u32[]{:S(2)}, u32[]{:S(2)}) collective-permute-start(f32[16,10,1]{2,1,0:T(8,128)S(1)} %get-tuple-element.7), channel_id=1, source_target_pairs={{0,1},{1,2},{2,3},{3,0},{4,5},{5,6},{6,7},{7,4},{8,9},{9,10},{10,1... | collective-permute-start | bytes 1928 | tf_op jit(solution)/shard_map/ppermute | solution.py:19
  21.7 8.5 %collective-permute-start.3 = (f32[16,10,1]{2,1,0:T(8,128)S(1)}, f32[16,10,1]{2,1,0:T(8,128)}, u32[]{:S(2)}, u32[]{:S(2)}) collective-permute-start(f32[16,10,1]{2,1,0:T(8,128)S(1)} %get-tuple-element.8), channel_id=1, source_target_pairs={{1,0},{2,1},{3,2},{0,3},{5,4},{6,5},{7,6},{4,7},{9,8},{10,9},{11,1... | collective-permute-start | bytes 1928 | tf_op jit(solution)/shard_map/ppermute | solution.py:22
  28.9 0.7 copy-start.3
  33.0 0.7 copy-start.4
  33.0 93.9 %all-reduce.5.cloned.1.call-start = ((), (), s32[]{:S(2)}) async-start(), calls=%async_computation.1 | async-start | bytes 262144 | tf_op jit(solution)/shard_map/psum | solution.py:90
  71.4 8.3 %collective-permute-start.5 = (f32[16,2,720]{2,1,0:T(2,128)S(1)}, f32[16,2,720]{2,1,0:T(2,128)S(1)}, u32[]{:S(2)}, u32[]{:S(2)}) collective-permute-start(f32[16,2,720]{2,1,0:T(2,128)S(1)} %pad_maximum_fusion.29), channel_id=1, source_target_pairs={{2,0},{3,1},{0,2},{1,3},{6,4},{7,5},{4,6},{5,7},{10,8},{11,9},{8,1... | collective-permute-start | bytes 276488 | tf_op jit(solution)/shard_map/ppermute | solution.py:30
  73.6 2.6 %collective-permute-start.6 = (f32[16,1,720]{2,1,0:T(1,128)S(1)}, f32[16,1,720]{2,1,0:T(1,128)S(1)}, u32[]{:S(2)}, u32[]{:S(2)}) collective-permute-start(f32[16,1,720]{2,1,0:T(1,128)S(1)} %get-tuple-element.9), channel_id=1, source_target_pairs={{0,4},{4,8},{8,12},{12,16},{16,20},{20,24},{24,28},{1,5},{5,9},{9,... | collective-permute-start | bytes 138248 | tf_op jit(solution)/shard_map/ppermute | solution.py:19
  74.9 4.9 %collective-permute-start.7 = (f32[16,1,720]{2,1,0:T(1,128)S(1)}, f32[16,1,720]{2,1,0:T(1,128)S(1)}, u32[]{:S(2)}, u32[]{:S(2)}) collective-permute-start(f32[16,1,720]{2,1,0:T(1,128)S(1)} %get-tuple-element.10), channel_id=1, source_target_pairs={{4,0},{8,4},{12,8},{16,12},{20,16},{24,20},{28,24},{5,1},{9,5},{13... | collective-permute-start | bytes 138248 | tf_op jit(solution)/shard_map/ppermute | solution.py:22
  80.0 6.9 %collective-permute-start.9 = (f32[16,10,1]{2,1,0:T(8,128)S(1)}, f32[16,10,1]{2,1,0:T(8,128)S(1)}, u32[]{:S(2)}, u32[]{:S(2)}) collective-permute-start(f32[16,10,1]{2,1,0:T(8,128)S(1)} %get-tuple-element.5), channel_id=1, source_target_pairs={{0,1},{1,2},{2,3},{3,0},{4,5},{5,6},{6,7},{7,4},{8,9},{9,10},{10,1... | collective-permute-start | bytes 1928 | tf_op jit(solution)/shard_map/ppermute | solution.py:19
  80.6 6.4 %collective-permute-start.8 = (f32[16,10,1]{2,1,0:T(8,128)S(1)}, f32[16,10,1]{2,1,0:T(8,128)S(1)}, u32[]{:S(2)}, u32[]{:S(2)}) collective-permute-start(f32[16,10,1]{2,1,0:T(8,128)S(1)} %get-tuple-element.6), channel_id=1, source_target_pairs={{1,0},{2,1},{3,2},{0,3},{5,4},{6,5},{7,6},{4,7},{9,8},{10,9},{11,1... | collective-permute-start | bytes 1928 | tf_op jit(solution)/shard_map/ppermute | solution.py:22
Sparse Core Ops, SparseCore 0:
  33.1 36.3 all-reduce.2
  89.0 37.8 all-reduce.4
where the time goes:
time: 136 us
  waiting for transfers between devices  86.4 us (64%)
  starting transfers between devices  22.5 us (17%)
  between operations  13.6 us (10%)
  matrix products  6.6 us (5%)
  other arithmetic  4.59 us (3%)
  local copies, waits for them, and re-layouts  2.6 us (2%)
    psum x2, waiting for transfers between devices, shards(): coefficients = lax.psum(partial_coeffs, 'lon')  73.7 us
    ppermute x4, starting transfers between devices, with_halo(): lax.ppermute(lax.slice_in_dim(block, 0, width, axis=dim), axis, backward)  8.73 us
    ppermute x4, starting transfers between devices, with_halo(): lax.ppermute(lax.slice_in_dim(block, block.shape[dim] - width, None, axis...  8.12 us
    ppermute x4, waiting for transfers between devices, with_halo(): lax.ppermute(lax.slice_in_dim(block, block.shape[dim] - width, None, axis...  7.37 us
    ppermute x2, starting transfers between devices, shifted(): return lax.ppermute(block, axis, route)  5.61 us
    ppermute x4, waiting for transfers between devices, with_halo(): lax.ppermute(lax.slice_in_dim(block, 0, width, axis=dim), axis, backward)  4.34 us
    dot_general x2, matrix products, shards(): filtered = jnp.dot(coefficients, synthesis, precision=lax.Precision.HIGHEST)  4.25 us
  transfers between devices with their start and end apart: 12, of which 8 were waited for; matrix products, arithmetic and copies ran while one was open for 1% of the time, Pallas kernels for 0%

commit v1 on v0

--- a/solution.py
+++ b/solution.py
@@ -87,7 +87,7 @@
         )
         flat_rows = tendency.reshape(flat_count, col_count)
         partial_coeffs = jnp.dot(flat_rows, analysis, precision=lax.Precision.HIGHEST)
-        coefficients = lax.psum(partial_coeffs, "lon")
+        coefficients = lax.all_gather(partial_coeffs, "lon").sum(axis=0)
         coefficients = coefficients * mode_mask(flat_cut)
         filtered = jnp.dot(coefficients, synthesis, precision=lax.Precision.HIGHEST)
         filtered = filtered.reshape(level_count, row_count, col_count)

time: 136 us -> 79.9 us (0.59)
  waiting for transfers between devices: 86.4 us -> 17.9 us
  blocking collectives: 0 us -> 31 us
  between operations: 13.6 us -> 0.22 us
  matrix products: 6.6 us -> 3.48 us
    psum x2 -> x0, waiting for transfers between devices: 73.7 us -> none  [shards(): coefficients = lax.psum(partial_coeffs, 'lon')]
    all_gather x0 -> x2, blocking collectives: none -> 31 us  [shards(): coefficients = lax.all_gather(partial_coeffs, 'lon').sum(axis=0)]
    ppermute x4, waiting for transfers between devices: 4.34 us -> 9.99 us  [with_halo(): lax.ppermute(lax.slice_in_dim(block, 0, width, axis=dim), axis, backward)]
    ppermute x4, starting transfers between devices: 8.12 us -> 11.5 us  [with_halo(): lax.ppermute(lax.slice_in_dim(block, block.shape[dim] - width, None, axis...]
    ppermute x4, starting transfers between devices: 8.73 us -> 5.47 us  [with_halo(): lax.ppermute(lax.slice_in_dim(block, 0, width, axis=dim), axis, backward)]
    dot_general x2, matrix products: 4.25 us -> 2.44 us  [shards(): filtered = jnp.dot(coefficients, synthesis, precision=lax.Precision.HIGHEST)]
    ppermute x2, starting transfers between devices: 5.61 us -> 4.23 us  [shifted(): return lax.ppermute(block, axis, route)]
  transfers between devices with their start and end apart: 12 -> 10, of which waited for: 8 -> 6; matrix products, arithmetic and copies ran while one was open for 1% -> 2% of each run, Pallas kernels for 0% -> 0%
where the time goes in v1:
time: 79.9 us; the launch traced here: 78.8 us
  blocking collectives  31 us (39%)
  starting transfers between devices  21.2 us (27%)
  waiting for transfers between devices  17.9 us (22%)
  other arithmetic  3.7 us (5%)
  matrix products  3.48 us (4%)
  local copies, waits for them, and re-layouts  1.37 us (2%)
    all_gather x2, blocking collectives, shards(): coefficients = lax.all_gather(partial_coeffs, 'lon').sum(axis=0)  31 us
    ppermute x4, starting transfers between devices, with_halo(): lax.ppermute(lax.slice_in_dim(block, block.shape[dim] - width, None, axis...  11.5 us
    ppermute x4, waiting for transfers between devices, with_halo(): lax.ppermute(lax.slice_in_dim(block, 0, width, axis=dim), axis, backward)  9.99 us
    ppermute x4, waiting for transfers between devices, with_halo(): lax.ppermute(lax.slice_in_dim(block, block.shape[dim] - width, None, axis...  7.02 us
    ppermute x4, starting transfers between devices, with_halo(): lax.ppermute(lax.slice_in_dim(block, 0, width, axis=dim), axis, backward)  5.47 us
    ppermute x2, starting transfers between devices, shifted(): return lax.ppermute(block, axis, route)  4.23 us
    dot_general x2, matrix products, shards(): filtered = jnp.dot(coefficients, synthesis, precision=lax.Precision.HIGHEST)  2.44 us
    mul x1, other arithmetic, fourier_tables(): cosine * weights[None, :]  1.62 us
  transfers between devices with their start and end apart: 10, of which 6 were waited for; matrix products, arithmetic and copies ran while one was open for 2% of the time, Pallas kernels for 0%

profile of v1, /device:TPU:0, one launch (start us, length us, event | category | flops | bytes accessed | tf_op | source)
XLA Modules:
  0.0 78.8 jit_solution(9373427743884090129)
XLA Ops:
  0.0 1.2 %fusion.28 = (f32[16,1,720]{2,1,0:T(1,128)S(1)}, f32[16,1,720]{2,1,0:T(1,128)S(1)}) fusion(f32[16,8,720]{2,1,0:T(8,128)} %param.4), kind=kLoop, calls=%fused_computation.72 | loop fusion | bytes 184320 | tf_op jit(solution)/shard_map/slice | solution.py:72
  1.2 2.4 %collective-permute-start.1 = (f32[16,1,720]{2,1,0:T(1,128)S(1)}, f32[16,1,720]{2,1,0:T(1,128)S(1)}, u32[]{:S(2)}, u32[]{:S(2)}) collective-permute-start(f32[16,1,720]{2,1,0:T(1,128)S(1)} %get-tuple-element.11), channel_id=1, source_target_pairs={{0,4},{4,8},{8,12},{12,16},{16,20},{20,24},{24,28},{1,5},{5,9},{9,... | collective-permute-start | bytes 138248 | tf_op jit(solution)/shard_map/ppermute | solution.py:19
  3.6 1.3 %collective-permute-start.2 = (f32[16,1,720]{2,1,0:T(1,128)S(1)}, f32[16,1,720]{2,1,0:T(1,128)S(1)}, u32[]{:S(2)}, u32[]{:S(2)}) collective-permute-start(f32[16,1,720]{2,1,0:T(1,128)S(1)} %get-tuple-element.12), channel_id=1, source_target_pairs={{4,0},{8,4},{12,8},{16,12},{20,16},{24,20},{28,24},{5,1},{9,5},{13... | collective-permute-start | bytes 138248 | tf_op jit(solution)/shard_map/ppermute | solution.py:22
  4.9 0.1 pad_maximum_fusion.28
  5.0 3.5 %collective-permute-start = (f32[16,2,720]{2,1,0:T(2,128)S(1)}, f32[16,2,720]{2,1,0:T(2,128)S(1)}, u32[]{:S(2)}, u32[]{:S(2)}) collective-permute-start(f32[16,2,720]{2,1,0:T(2,128)S(1)} %pad_maximum_fusion.28), channel_id=1, source_target_pairs={{2,0},{3,1},{0,2},{1,3},{6,4},{7,5},{4,6},{5,7},{10,8},{11,9},{8,1... | collective-permute-start | bytes 276488 | tf_op jit(solution)/shard_map/ppermute | solution.py:30
  8.5 1.6 %broadcast_multiply_fusion.1 = (f32[720,128]{1,0:T(8,128)S(1)}, f32[720,128]{1,0:T(8,128)S(1)}, f32[720,128]{1,0:T(8,128)S(1)}, f32[720,128]{1,0:T(8,128)S(1)}) fusion(f32[128]{0:T(128)S(1)} %compare_select_fusion.4, s32[720]{0:T(1024)S(1)} %iota_add_fusion), kind=kLoop, calls=%fused_computation.40 | loop fusion | flops 1013760 | bytes 1477952 | tf_op jit(solution)/shard_map/mul | solution.py:40
  10.2 0.9 %collective-permute-done = f32[16,2,720]{2,1,0:T(2,128)S(1)} collective-permute-done((f32[16,2,720]{2,1,0:T(2,128)S(1)}, f32[16,2,720]{2,1,0:T(2,128)S(1)}, u32[]{:S(2)}, u32[]{:S(2)}) %collective-permute-start) | collective-permute-done | bytes 92192 | tf_op jit(solution)/shard_map/ppermute | solution.py:30
  11.1 0.1 broadcast_select_fusion.3
  11.2 0.1 pad_maximum_fusion.25
  11.4 3.8 %collective-permute-start.4 = (f32[16,10,1]{2,1,0:T(8,128)S(1)}, f32[16,10,1]{2,1,0:T(8,128)S(1)}, u32[]{:S(2)}, u32[]{:S(2)}) collective-permute-start(f32[16,10,1]{2,1,0:T(8,128)S(1)} %get-tuple-element.7), channel_id=1, source_target_pairs={{0,1},{1,2},{2,3},{3,0},{4,5},{5,6},{6,7},{7,4},{8,9},{9,10},{10,1... | collective-permute-start | bytes 1928 | tf_op jit(solution)/shard_map/ppermute | solution.py:19
  15.2 2.9 %collective-permute-start.3 = (f32[16,10,1]{2,1,0:T(8,128)S(1)}, f32[16,10,1]{2,1,0:T(8,128)S(1)}, u32[]{:S(2)}, u32[]{:S(2)}) collective-permute-start(f32[16,10,1]{2,1,0:T(8,128)S(1)} %get-tuple-element.8), channel_id=1, source_target_pairs={{1,0},{2,1},{3,2},{0,3},{5,4},{6,5},{7,6},{4,7},{9,8},{10,9},{11,1... | collective-permute-start | bytes 1928 | tf_op jit(solution)/shard_map/ppermute | solution.py:22
  18.2 0.1 lt.38
  18.2 4.2 %collective-permute-done.4 = f32[16,10,1]{2,1,0:T(8,128)S(1)} collective-permute-done((f32[16,10,1]{2,1,0:T(8,128)S(1)}, f32[16,10,1]{2,1,0:T(8,128)S(1)}, u32[]{:S(2)}, u32[]{:S(2)}) %collective-permute-start.4) | collective-permute-done | bytes 672 | tf_op jit(solution)/shard_map/ppermute | solution.py:19
  22.4 1.2 %collective-permute-done.3 = f32[16,10,1]{2,1,0:T(8,128)S(1)} collective-permute-done((f32[16,10,1]{2,1,0:T(8,128)S(1)}, f32[16,10,1]{2,1,0:T(8,128)S(1)}, u32[]{:S(2)}, u32[]{:S(2)}) %collective-permute-start.3) | collective-permute-done | bytes 672 | tf_op jit(solution)/shard_map/ppermute | solution.py:22
  23.6 0.6 multiply_add_fusion.1
  24.2 0.5 fusion.5
  24.7 15.3 %all-gather = f32[512,256]{1,0:T(8,128)S(1)} all-gather(f32[128,256]{1,0:T(8,128)S(1)} %fusion.5), channel_id=2, replica_groups=mesh['lat'=8,'lon'=4] {'lon'}, dimensions={0}, use_global_device_ids=true | all-gather | bytes 655360 | tf_op jit(solution)/shard_map/all_gather | solution.py:90
  40.1 0.8 %fusion.1 = f32[16,8,720]{2,1,0:T(8,128)S(1)} fusion(f32[16,8,720]{2,1,0:T(8,128)S(1)} %copy-done, f32[16,8,720]{2,1,0:T(8,128)S(1)} %multiply_add_fusion.1, f32[720,128]{1,0:T(8,128)S(1)} %get-tuple-element.19, f32[720,128]{1,0:T(8,128)S(1)} %get-tuple-element.20, pred[]{:T(512)S(6)} %or.3, f32[128,256]{1,0:T(8,128)S(1)} %reduce_sum.18, ...), kind=kOutput, calls=%fused_computation.3 | convolution fusion | flops 283549696 | bytes 1975809 | tf_op jit(solution)/shard_map/dot_general | solution.py:92
  41.0 0.1 pad_maximum_fusion.29
  41.1 0.8 collective-permute-start.5
  41.8 1.3 %collective-permute-start.6 = (f32[16,1,720]{2,1,0:T(1,128)S(1)}, f32[16,1,720]{2,1,0:T(1,128)S(1)}, u32[]{:S(2)}, u32[]{:S(2)}) collective-permute-start(f32[16,1,720]{2,1,0:T(1,128)S(1)} %get-tuple-element.9), channel_id=1, source_target_pairs={{0,4},{4,8},{8,12},{12,16},{16,20},{20,24},{24,28},{1,5},{5,9},{9,... | collective-permute-start | bytes 138248 | tf_op jit(solution)/shard_map/ppermute | solution.py:19
  43.1 1.3 %collective-permute-start.7 = (f32[16,1,720]{2,1,0:T(1,128)S(1)}, f32[16,1,720]{2,1,0:T(1,128)S(1)}, u32[]{:S(2)}, u32[]{:S(2)}) collective-permute-start(f32[16,1,720]{2,1,0:T(1,128)S(1)} %get-tuple-element.10), channel_id=1, source_target_pairs={{4,0},{8,4},{12,8},{16,12},{20,16},{24,20},{28,24},{5,1},{9,5},{13... | collective-permute-start | bytes 138248 | tf_op jit(solution)/shard_map/ppermute | solution.py:22
  44.4 4.8 %collective-permute-done.7 = f32[16,1,720]{2,1,0:T(1,128)S(1)} collective-permute-done((f32[16,1,720]{2,1,0:T(1,128)S(1)}, f32[16,1,720]{2,1,0:T(1,128)S(1)}, u32[]{:S(2)}, u32[]{:S(2)}) %collective-permute-start.7) | collective-permute-done | bytes 46112 | tf_op jit(solution)/shard_map/ppermute | solution.py:22
  49.2 0.1 broadcast_select_fusion.2
  49.4 0.1 pad_maximum_fusion.22
  49.5 4.0 %collective-permute-start.9 = (f32[16,10,1]{2,1,0:T(8,128)S(1)}, f32[16,10,1]{2,1,0:T(8,128)S(1)}, u32[]{:S(2)}, u32[]{:S(2)}) collective-permute-start(f32[16,10,1]{2,1,0:T(8,128)S(1)} %get-tuple-element.5), channel_id=1, source_target_pairs={{0,1},{1,2},{2,3},{3,0},{4,5},{5,6},{6,7},{7,4},{8,9},{9,10},{10,1... | collective-permute-start | bytes 1928 | tf_op jit(solution)/shard_map/ppermute | solution.py:19
  53.5 2.9 %collective-permute-done.9 = f32[16,10,1]{2,1,0:T(8,128)S(1)} collective-permute-done((f32[16,10,1]{2,1,0:T(8,128)S(1)}, f32[16,10,1]{2,1,0:T(8,128)S(1)}, u32[]{:S(2)}, u32[]{:S(2)}) %collective-permute-start.9) | collective-permute-done | bytes 672 | tf_op jit(solution)/shard_map/ppermute | solution.py:19
  56.3 4.0 %collective-permute-done.8 = f32[16,10,1]{2,1,0:T(8,128)S(1)} collective-permute-done((f32[16,10,1]{2,1,0:T(8,128)S(1)}, f32[16,10,1]{2,1,0:T(8,128)S(1)}, u32[]{:S(2)}, u32[]{:S(2)}) %collective-permute-start.8) | collective-permute-done | bytes 672 | tf_op jit(solution)/shard_map/ppermute | solution.py:22
  60.3 0.6 multiply_add_fusion
  61.0 0.5 fusion.4
  61.5 15.7 %all-gather.1 = f32[512,256]{1,0:T(8,128)S(1)} all-gather(f32[128,256]{1,0:T(8,128)S(1)} %fusion.4), channel_id=3, replica_groups=mesh['lat'=8,'lon'=4] {'lon'}, dimensions={0}, use_global_device_ids=true | all-gather | bytes 655360 | tf_op jit(solution)/shard_map/all_gather | solution.py:90
  77.2 1.6 %fusion.3 = f32[16,8,720]{2,1,0:T(8,128)} fusion(f32[16,8,720]{2,1,0:T(8,128)S(1)} %fusion.1, f32[16,8,720]{2,1,0:T(8,128)S(1)} %multiply_add_fusion, f32[720,128]{1,0:T(8,128)S(1)} %get-tuple-element.19, f32[720,128]{1,0:T(8,128)S(1)} %get-tuple-element.20, pred[]{:T(512)S(6)} %or.3, f32[128,256]{1,0:T(8,128)S(1)} %reduce_sum.19, ...), kind=kOutput, calls=%fused_computation.5 | convolution fusion | flops 283549696 | bytes 1975809 | tf_op jit(solution)/shard_map/dot_general | solution.py:92
  (26 shorter events, 0.3 us)
Async XLA Ops:
  1.2 9.0 %collective-permute-start.1 = (f32[16,1,720]{2,1,0:T(1,128)S(1)}, f32[16,1,720]{2,1,0:T(1,128)S(1)}, u32[]{:S(2)}, u32[]{:S(2)}) collective-permute-start(f32[16,1,720]{2,1,0:T(1,128)S(1)} %get-tuple-element.11), channel_id=1, source_target_pairs={{0,4},{4,8},{8,12},{12,16},{16,20},{20,24},{24,28},{1,5},{5,9},{9,... | collective-permute-start | bytes 138248 | tf_op jit(solution)/shard_map/ppermute | solution.py:19
  3.6 6.6 %collective-permute-start.2 = (f32[16,1,720]{2,1,0:T(1,128)S(1)}, f32[16,1,720]{2,1,0:T(1,128)S(1)}, u32[]{:S(2)}, u32[]{:S(2)}) collective-permute-start(f32[16,1,720]{2,1,0:T(1,128)S(1)} %get-tuple-element.12), channel_id=1, source_target_pairs={{4,0},{8,4},{12,8},{16,12},{20,16},{24,20},{28,24},{5,1},{9,5},{13... | collective-permute-start | bytes 138248 | tf_op jit(solution)/shard_map/ppermute | solution.py:22
  5.0 6.1 %collective-permute-start = (f32[16,2,720]{2,1,0:T(2,128)S(1)}, f32[16,2,720]{2,1,0:T(2,128)S(1)}, u32[]{:S(2)}, u32[]{:S(2)}) collective-permute-start(f32[16,2,720]{2,1,0:T(2,128)S(1)} %pad_maximum_fusion.28), channel_id=1, source_target_pairs={{2,0},{3,1},{0,2},{1,3},{6,4},{7,5},{4,6},{5,7},{10,8},{11,9},{8,1... | collective-permute-start | bytes 276488 | tf_op jit(solution)/shard_map/ppermute | solution.py:30
  8.5 2.7 %copy-start = (f32[16,8,720]{2,1,0:T(8,128)S(1)}, f32[16,8,720]{2,1,0:T(8,128)}, u32[]{:S(2)}) copy-start(f32[16,8,720]{2,1,0:T(8,128)} %param.4) | copy-start | bytes 1105924
  11.1 12.6 %copy-start.3 = (f32[16,8,720]{2,1,0:T(8,128)S(1)}, f32[16,8,720]{2,1,0:T(8,128)}, u32[]{:S(2)}) copy-start(f32[16,8,720]{2,1,0:T(8,128)} %param.5) | copy-start | bytes 1105924
  11.2 12.4 %copy-start.1 = (f32[16,8,720]{2,1,0:T(8,128)S(1)}, f32[16,8,720]{2,1,0:T(8,128)}, u32[]{:S(2)}) copy-start(f32[16,8,720]{2,1,0:T(8,128)} %param.6) | copy-start | bytes 1105924
  11.4 6.7 %copy-start.5 = (s32[16]{0:T(128)S(1)}, s32[16]{0:T(128)}, u32[]{:S(2)}) copy-start(s32[16]{0:T(128)} %param.7) | copy-start | bytes 196
  11.4 11.0 %collective-permute-start.4 = (f32[16,10,1]{2,1,0:T(8,128)S(1)}, f32[16,10,1]{2,1,0:T(8,128)S(1)}, u32[]{:S(2)}, u32[]{:S(2)}) collective-permute-start(f32[16,10,1]{2,1,0:T(8,128)S(1)} %get-tuple-element.7), channel_id=1, source_target_pairs={{0,1},{1,2},{2,3},{3,0},{4,5},{5,6},{6,7},{7,4},{8,9},{9,10},{10,1... | collective-permute-start | bytes 1928 | tf_op jit(solution)/shard_map/ppermute | solution.py:19
  15.2 8.4 %collective-permute-start.3 = (f32[16,10,1]{2,1,0:T(8,128)S(1)}, f32[16,10,1]{2,1,0:T(8,128)S(1)}, u32[]{:S(2)}, u32[]{:S(2)}) collective-permute-start(f32[16,10,1]{2,1,0:T(8,128)S(1)} %get-tuple-element.8), channel_id=1, source_target_pairs={{1,0},{2,1},{3,2},{0,3},{5,4},{6,5},{7,6},{4,7},{9,8},{10,9},{11,1... | collective-permute-start | bytes 1928 | tf_op jit(solution)/shard_map/ppermute | solution.py:22
  41.1 8.1 %collective-permute-start.5 = (f32[16,2,720]{2,1,0:T(2,128)S(1)}, f32[16,2,720]{2,1,0:T(2,128)S(1)}, u32[]{:S(2)}, u32[]{:S(2)}) collective-permute-start(f32[16,2,720]{2,1,0:T(2,128)S(1)} %pad_maximum_fusion.29), channel_id=1, source_target_pairs={{2,0},{3,1},{0,2},{1,3},{6,4},{7,5},{4,6},{5,7},{10,8},{11,9},{8,1... | collective-permute-start | bytes 276488 | tf_op jit(solution)/shard_map/ppermute | solution.py:30
  41.8 2.6 %collective-permute-start.6 = (f32[16,1,720]{2,1,0:T(1,128)S(1)}, f32[16,1,720]{2,1,0:T(1,128)S(1)}, u32[]{:S(2)}, u32[]{:S(2)}) collective-permute-start(f32[16,1,720]{2,1,0:T(1,128)S(1)} %get-tuple-element.9), channel_id=1, source_target_pairs={{0,4},{4,8},{8,12},{12,16},{16,20},{20,24},{24,28},{1,5},{5,9},{9,... | collective-permute-start | bytes 138248 | tf_op jit(solution)/shard_map/ppermute | solution.py:19
  43.1 6.1 %collective-permute-start.7 = (f32[16,1,720]{2,1,0:T(1,128)S(1)}, f32[16,1,720]{2,1,0:T(1,128)S(1)}, u32[]{:S(2)}, u32[]{:S(2)}) collective-permute-start(f32[16,1,720]{2,1,0:T(1,128)S(1)} %get-tuple-element.10), channel_id=1, source_target_pairs={{4,0},{8,4},{12,8},{16,12},{20,16},{24,20},{28,24},{5,1},{9,5},{13... | collective-permute-start | bytes 138248 | tf_op jit(solution)/shard_map/ppermute | solution.py:22
  49.2 11.1 %copy-start.4 = (f32[16,8,720]{2,1,0:T(8,128)S(1)}, f32[16,8,720]{2,1,0:T(8,128)}, u32[]{:S(2)}) copy-start(f32[16,8,720]{2,1,0:T(8,128)} %param.5) | copy-start | bytes 1105924
  49.3 11.0 %copy-start.2 = (f32[16,8,720]{2,1,0:T(8,128)S(1)}, f32[16,8,720]{2,1,0:T(8,128)}, u32[]{:S(2)}) copy-start(f32[16,8,720]{2,1,0:T(8,128)} %param.6) | copy-start | bytes 1105924
  49.5 6.8 %collective-permute-start.9 = (f32[16,10,1]{2,1,0:T(8,128)S(1)}, f32[16,10,1]{2,1,0:T(8,128)S(1)}, u32[]{:S(2)}, u32[]{:S(2)}) collective-permute-start(f32[16,10,1]{2,1,0:T(8,128)S(1)} %get-tuple-element.5), channel_id=1, source_target_pairs={{0,1},{1,2},{2,3},{3,0},{4,5},{5,6},{6,7},{7,4},{8,9},{9,10},{10,1... | collective-permute-start | bytes 1928 | tf_op jit(solution)/shard_map/ppermute | solution.py:19
  53.4 6.9 %collective-permute-start.8 = (f32[16,10,1]{2,1,0:T(8,128)S(1)}, f32[16,10,1]{2,1,0:T(8,128)S(1)}, u32[]{:S(2)}, u32[]{:S(2)}) collective-permute-start(f32[16,10,1]{2,1,0:T(8,128)S(1)} %get-tuple-element.6), channel_id=1, source_target_pairs={{1,0},{2,1},{3,2},{0,3},{5,4},{6,5},{7,6},{4,7},{9,8},{10,9},{11,1... | collective-permute-start | bytes 1928 | tf_op jit(solution)/shard_map/ppermute | solution.py:22
